TPU v7x, 128 devices: a whole 4x4x4 slice. The times are simulated.
128 devices in a mesh: dp: 2 (over z_hi), seq: 32 (over y, x, core), tensor: 2 (over z_lo).
Axes of the slice: x: 4, y: 4, z: 4 (z_hi: 2, z_lo: 2; z = z_hi * 2 + z_lo), core: 2. Of those that a mesh axis runs over, the one named last changes fastest.
Arguments:
- queries: bfloat16 [2, 16384, 4096], P('dp', 'seq', 'tensor'), may hold values from -6 to 6
- keys: bfloat16 [2, 16384, 4096], P('dp', 'seq', 'tensor'), may hold values from -6 to 6
- values: bfloat16 [2, 16384, 4096], P('dp', 'seq', 'tensor'), may hold values from -40 to 40
- grad_out: bfloat16 [2, 16384, 4096], P('dp', 'seq', 'tensor'), may hold values from -48 to 48
- doc_lengths: int32 [2, 16], P('dp'), may hold values from 1 to 9216, 16384 in all within a row
- gain: float32 [4096], P('tensor'), may hold values from 0.1 to 1.9
Outputs:
- layer_out: bfloat16 [2, 16384, 4096], P('dp', 'seq', 'tensor')
- grad_queries: bfloat16 [2, 16384, 4096], P('dp', 'seq', 'tensor')
- grad_keys: bfloat16 [2, 16384, 4096], P('dp', 'seq', 'tensor')
- grad_values: bfloat16 [2, 16384, 4096], P('dp', 'seq', 'tensor')
- grad_gain: float32 [4096], P('tensor')
Inputs may be any that keep to these rules, and one draw needn't show every extreme that they name: `doc_lengths`: each row sums to 16384; in every sequence the longest document has exactly 9216 tokens.
All inputs are finite; a program needn't handle non-finite values.
Results may differ from a plain program's by a relative error of at most 0.0063.
Values may be sent and summed in bfloat16 or wider, within the bound.
No kernel may reach another device: no remote copies, remote signals or barrier semaphores. Data moves between devices by JAX's collectives and lax.ppermute only.
A program may use at most 128 MiB of HBM per device.

v0:
```python
import jax
import jax.numpy as jnp
from jax import lax
from jax.sharding import PartitionSpec as P

HEADS = 32
HD = 128
epsilon = 1e-05


def prefix(value, axis, join, neutral, backward):
    count = lax.axis_size(axis)
    place = lax.axis_index(axis)
    ahead = count - 1 - place if backward else place
    gathered = jax.tree.map(
        lambda a, kind: lax.all_gather(a.astype(kind), axis), value, (jnp.bfloat16, jnp.bfloat16)
    )
    state = jax.tree.map(lambda a, e: jnp.zeros_like(a) + jnp.asarray(e, a.dtype), value, neutral)

    def one(step, state):
        source = count - 1 - step if backward else step
        return join(
            state,
            jax.tree.map(
                lambda a, own: lax.dynamic_index_in_dim(a, source, 0, False).astype(own.dtype),
                gathered,
                value,
            ),
        )

    return lax.fori_loop(0, ahead, one, state)


def linked(earlier, later):
    keeping = 1.0 - later[1][0]
    return (later[0] + keeping * earlier[0], jnp.maximum(earlier[1], later[1]))


def carried(state, flags, backward):
    blank = jnp.zeros(state.shape, jnp.float32)
    total, unused = prefix(
        (state.astype(jnp.float32), flags),
        "seq",
        linked,
        (blank, jnp.zeros((1,), jnp.float32)),
        backward,
    )
    return total


def head_major(array, shape):
    return jnp.transpose(array.reshape(shape), (1, 0, 2))


def body(queries, keys, values, grad_out, doc_lengths, gain):
    count = queries.shape[1]
    local_width = queries.shape[2]
    local_heads = local_width // HD
    shape = (count, local_heads, HD)
    query = head_major(queries[0], shape)
    key = head_major(keys[0], shape)
    value = head_major(values[0], shape)
    lengths = doc_lengths[0]
    starts = jnp.cumsum(lengths) - lengths
    block = lax.axis_index("seq")
    begin = block * count
    position = begin + jnp.arange(count, dtype=jnp.int32)
    document = jnp.sum((starts[None, :] <= position[:, None]).astype(jnp.int32), axis=1) - 1
    first_doc = document[0]
    last_doc = document[-1]
    numbers = jnp.arange(starts.shape[0], dtype=jnp.int32)
    last_end = jnp.sum(jnp.where(numbers == last_doc, starts + lengths, 0))
    last_block = (last_end - 1) // count
    continues = jnp.logical_not(jnp.any(starts == begin))
    starts_here = jnp.any((starts >= begin) & (starts < begin + count))
    flags = starts_here.astype(jnp.float32).reshape(1)
    first_mask = (document == first_doc) & continues
    last_mask = document == last_doc
    indices = jnp.arange(count, dtype=jnp.int32)
    same = (indices[:, None] >= indices[None, :]) & (document[:, None] == document[None, :])
    key_last = jnp.where(last_mask[None, :, None], key, 0)
    value_last = jnp.where(last_mask[None, :, None], value, 0)
    query_first = jnp.where(first_mask[None, :, None], query, 0)
    state = jnp.einsum("htd,hte->hde", key_last, value, preferred_element_type=jnp.float32).astype(
        jnp.bfloat16
    )
    incoming = carried(state, flags, False)
    carry_in = jnp.where(continues, incoming, 0.0).astype(jnp.bfloat16)
    scores = jnp.einsum("htd,hsd->hts", query, key, preferred_element_type=jnp.float32)
    scores = jnp.where(same[None], scores, 0.0).astype(jnp.bfloat16)
    attended = jnp.einsum("hts,hsd->htd", scores, value, preferred_element_type=jnp.float32)
    attended = attended + jnp.einsum(
        "htd,hde->hte", query_first, carry_in, preferred_element_type=jnp.float32
    )
    attended = jnp.transpose(attended, (1, 0, 2)).reshape(count, local_width)
    squares = lax.psum(jnp.sum(attended * attended, axis=1), "tensor")
    rscale = lax.rsqrt(squares / (HEADS * HD) + epsilon)
    unit = attended * rscale[:, None]
    layer_out = (gain * unit).astype(jnp.bfloat16)
    upstream = grad_out[0].astype(jnp.float32)
    scaled = upstream * gain
    inner = lax.psum(jnp.sum(scaled * unit, axis=1), "tensor") / (HEADS * HD)
    grad_gain = lax.psum(jnp.sum(upstream * unit, axis=0), ("dp", "seq"))
    d_att = head_major(
        (rscale[:, None] * (scaled - unit * inner[:, None])).astype(jnp.bfloat16), shape
    )
    d_first = jnp.where(first_mask[None, :, None], d_att, 0)
    back_state = jnp.einsum(
        "htd,hte->hde", query_first, d_att, preferred_element_type=jnp.float32
    ).astype(jnp.bfloat16)
    outgoing = carried(back_state, flags, True)
    carry_back = jnp.where(last_block > block, outgoing, 0.0).astype(jnp.bfloat16)
    d_scores = jnp.einsum("hte,hse->hts", d_att, value, preferred_element_type=jnp.float32)
    d_scores = jnp.where(same[None], d_scores, 0.0).astype(jnp.bfloat16)
    grad_query = jnp.einsum("hts,hsd->htd", d_scores, key, preferred_element_type=jnp.float32)
    grad_query = grad_query + jnp.einsum(
        "hte,hde->htd", d_first, carry_in, preferred_element_type=jnp.float32
    )
    grad_key = jnp.einsum("hts,htd->hsd", d_scores, query, preferred_element_type=jnp.float32)
    grad_key = grad_key + jnp.einsum(
        "hse,hde->hsd", value_last, carry_back, preferred_element_type=jnp.float32
    )
    grad_value = jnp.einsum("hts,hte->hse", scores, d_att, preferred_element_type=jnp.float32)
    grad_value = grad_value + jnp.einsum(
        "hsd,hde->hse", key_last, carry_back, preferred_element_type=jnp.float32
    )
    out_shape = (1, count, local_width)

    def token_major(array):
        return jnp.transpose(array.astype(jnp.bfloat16), (1, 0, 2)).reshape(out_shape)

    return (
        layer_out.reshape(out_shape),
        token_major(grad_query),
        token_major(grad_key),
        token_major(grad_value),
        grad_gain,
    )


def solution(mesh):
    in_specs = (
        P("dp", "seq", "tensor"),
        P("dp", "seq", "tensor"),
        P("dp", "seq", "tensor"),
        P("dp", "seq", "tensor"),
        P("dp", None),
        P("tensor"),
    )
    out_specs = (
        P("dp", "seq", "tensor"),
        P("dp", "seq", "tensor"),
        P("dp", "seq", "tensor"),
        P("dp", "seq", "tensor"),
        P("tensor"),
    )
    return jax.shard_map(body, mesh=mesh, in_specs=in_specs, out_specs=out_specs, check_vma=False)
```

profile of v0, /device:TPU:0, one launch (start us, length us, event | category | flops | bytes accessed | tf_op | source)
XLA Modules:
  0.0 547.0 jit_solution(15308874766064887949)
XLA Ops:
  11.5 3.9 copy.79
  15.4 2.9 copy.82
  19.6 3.1 fusion.16
  24.8 69.2 %all-reduce = bf16[32]{0:T(256)(128)(2,1)S(1)} all-reduce(bf16[32]{0:T(256)(128)(2,1)S(1)} %dynamic-update-slice), channel_id=1, replica_groups=mesh['dp'=2,'seq'=32,'tensor'=2] {'seq'}, use_global_device_ids=true, to_apply=%add | all-reduce | flops 32 | bytes 128
  94.1 2.9 copy.78
  97.0 4.1 copy.87
  101.3 4.2 select_convert_fusion.1
  105.5 3.2 copy-done.1
  108.7 4.8 fusion.40
  113.6 5.0 fusion.7
  118.6 5.0 psum.21
  123.6 5.4 copy.88
  129.0 4.0 fusion.2
  133.0 5.1 psum.22
  138.2 4.3 fusion.8
  147.3 5.4 copy.86
  152.7 4.8 select_convert_fusion
  157.6 4.8 fusion.41
  162.4 4.3 add_convert_fusion.2
  166.7 3.9 copy.96
  170.6 252.2 %psum.23 = f32[2048]{0:T(1024)} all-reduce(f32[2048]{0:T(1024)S(1)} %get-tuple-element.155), channel_id=1, replica_groups=mesh['dp'=2,'seq'=32,'tensor'=2] {'dp','seq'}, use_global_device_ids=true, to_apply=%region_14.15 | all-reduce | flops 2048 | bytes 16384 | tf_op jit(solution)/shard_map/psum | solution.py:103
  422.8 3.9 multiply_convert_fusion
  426.7 6.7 %fusion.42 = f32[16,512,128]{1,2,0:T(8,128)} fusion(bf16[16,512,128]{1,2,0:T(8,128)(2,1)S(1)} %bitcast.105, bf16[16,512,512]{2,1,0:T(8,128)(2,1)} %copy-done), kind=kOutput, calls=%fused_computation.74 | convolution fusion | flops 1073741824 | bytes 14680064 | tf_op jit(solution)/shard_map/hts,htd->hsd/dot_general | solution.py:119
  433.5 86.6 %while.27 = (s32[]{:T(128)}, f32[16,128,128]{2,1,0:T(8,128)S(1)}, s32[]{:T(128)}, bf16[32,16,128,128]{3,2,1,0:T(8,128)(2,1)}, bf16[32,1]{0,1:T(2,128)(2,1)S(1)},...) while((s32[]{:T(128)}, f32[16,128,128]{2,1,0:T(8,128)S(1)}, s32[]{:T(128)}, ...), condition=%wide.region_12.13_spmd, body=%wide.region_11.12_spmd.sunk | while | flops 786439 | bytes 2621605 | solution.py:31
  434.2 2.1 convert_add_fusion.5
  437.0 2.1 convert_add_fusion.5
  439.8 2.1 convert_add_fusion.5
  442.6 2.1 convert_add_fusion.5
  445.4 2.1 convert_add_fusion.5
  448.1 2.1 convert_add_fusion.5
  450.9 2.1 convert_add_fusion.5
  453.7 2.1 convert_add_fusion.5
  456.5 2.1 convert_add_fusion.5
  459.3 2.1 convert_add_fusion.5
  462.1 2.1 convert_add_fusion.5
  464.9 2.1 convert_add_fusion.5
  467.7 2.1 convert_add_fusion.5
  470.4 2.1 convert_add_fusion.5
  473.2 2.1 convert_add_fusion.5
  476.0 2.1 convert_add_fusion.5
  478.8 2.1 convert_add_fusion.5
  481.6 2.1 convert_add_fusion.5
  484.4 2.1 convert_add_fusion.5
  487.2 2.1 convert_add_fusion.5
  521.8 6.2 %add_convert_fusion = bf16[16,512,128]{1,2,0:T(8,128)(2,1)} fusion(f32[16,512,128]{1,2,0:T(8,128)S(1)} %fusion.14, bf16[16,512,128]{1,2,0:T(8,128)(2,1)S(1)} %copy-done.9, bf16[16,512,512]{2,1,0:T(8,128)(2,1)} %copy-done.1), kind=kOutput, calls=%fused_computation.18 | convolution fusion | flops 1075838976 | bytes 16777216 | tf_op jit(solution)/shard_map/hts,hte->hse/dot_general | solution.py:123
  528.0 4.1 copy.98
  532.1 4.2 add_convert_fusion.1
  536.3 3.9 copy.97
  (93 shorter events, 56.2 us)
Async XLA Ops:
  7.2 106.3 %all-gather.5.cloned.1.call-start = ((), (), s32[]{:S(2)}) async-start(), calls=%async_computation | async-start | bytes 17301504 | tf_op jit(solution)/shard_map/all_gather | solution.py:16
  18.3 4.5 copy-start.2
  19.6 3.9 copy-start.11
  22.8 410.6 %all-gather.7.cloned.1.call-start = ((), (), s32[]{:S(2)}) async-start(), calls=%async_computation.1 | async-start | bytes 17301504 | tf_op jit(solution)/shard_map/all_gather | solution.py:16
  101.3 7.4 %copy-start.3 = (bf16[1,512,2048]{1,2,0:T(8,128)(2,1)S(1)}, bf16[1,512,2048]{1,2,0:T(8,128)(2,1)}, u32[]{:S(2)}) copy-start(bf16[1,512,2048]{1,2,0:T(8,128)(2,1)} %copy-done.2) | copy-start | bytes 6291460
  105.5 3.2 copy-start.1
  123.6 5.4 copy-start.10
  142.4 1.4 copy-start.7
  152.7 4.8 copy-start.5
  157.6 4.8 copy-start
  157.6 4.8 copy-start.8
  433.5 86.7 %copy-start.6 = (bf16[1,512,2048]{1,2,0:T(8,128)(2,1)S(1)}, bf16[1,512,2048]{1,2,0:T(8,128)(2,1)}, u32[]{:S(2)}) copy-start(bf16[1,512,2048]{1,2,0:T(8,128)(2,1)} %copy.79) | copy-start | bytes 6291460
  520.2 1.6 copy-start.9
  528.0 4.1 copy-start.4
Sparse Core Ops, SparseCore 0:
  22.9 75.2 all-gather.4
  145.5 151.3 all-gather.6
where the time goes:
time: 550 us; the launch traced here: 547 us
  blocking collectives  332 us (60%)
  other arithmetic  103 us (19%)
  matrix products  50.3 us (9%)
  local copies, waits for them, and re-layouts  44.8 us (8%)
  between operations  16.2 us (3%)
    psum x1, blocking collectives, body(): grad_gain = lax.psum(jnp.sum(upstream * unit, axis=0), ('dp', 'seq'))  252 us
    unnamed x1, blocking collectives  69.2 us
    add x31, other arithmetic, linked(): return (later[0] + keeping * earlier[0], jnp.maximum(earlier[1], later[1]))  65.4 us
    unnamed x33, local copies, waits for them, and re-layouts  28.3 us
    sub x31, other arithmetic, linked(): keeping = 1.0 - later[1][0]  20.3 us
  transfers between devices with their start and end apart: 2, of which 0 were waited for; matrix products, arithmetic and copies ran while one was open for 10% of the time, Pallas kernels for 0%

commit v1 on v0

--- a/solution.py
+++ b/solution.py
@@ -1,3 +1,4 @@
+import functools
 import jax
 import jax.numpy as jnp
 from jax import lax
@@ -6,6 +7,14 @@
 HEADS = 32
 HD = 128
 epsilon = 1e-05
+
+
+def replace_values(base_x, row_axis, a_name):
+    near = lax.psum(base_x, row_axis)
+    return lax.psum(near, a_name)
+
+
+solve_the_chunk = functools.partial(replace_values, row_axis="dp", a_name="seq")
 
 
 def prefix(value, axis, join, neutral, backward):
@@ -100,7 +109,7 @@
     upstream = grad_out[0].astype(jnp.float32)
     scaled = upstream * gain
     inner = lax.psum(jnp.sum(scaled * unit, axis=1), "tensor") / (HEADS * HD)
-    grad_gain = lax.psum(jnp.sum(upstream * unit, axis=0), ("dp", "seq"))
+    grad_gain = solve_the_chunk(jnp.sum(upstream * unit, axis=0))
     d_att = head_major(
         (rscale[:, None] * (scaled - unit * inner[:, None])).astype(jnp.bfloat16), shape
     )

time: 550 us -> 452 us (0.82)
  blocking collectives: 332 us -> 234 us
    psum x1 -> x2, blocking collectives: 252 us -> 155 us  [the longest x1 148 us: replace_values(): return lax.psum(near, a_name)]
  transfers between devices with their start and end apart: 2 -> 2, of which waited for: 0 -> 0; matrix products, arithmetic and copies ran while one was open for 10% -> 12% of each run, Pallas kernels for 0% -> 0%
where the time goes in v1:
time: 452 us; the launch traced here: 449 us
  blocking collectives  234 us (52%)
  other arithmetic  103 us (23%)
  matrix products  50.3 us (11%)
  local copies, waits for them, and re-layouts  44.8 us (10%)
  between operations  16.2 us (4%)
    psum x1, blocking collectives, replace_values(): return lax.psum(near, a_name)  148 us
    unnamed x1, blocking collectives  69.2 us
    add x31, other arithmetic, linked(): return (later[0] + keeping * earlier[0], jnp.maximum(earlier[1], later[1]))  65.4 us
    unnamed x33, local copies, waits for them, and re-layouts  28.3 us
    sub x31, other arithmetic, linked(): keeping = 1.0 - later[1][0]  20.3 us
    reshape x2, local copies, waits for them, and re-layouts, body(): attended = jnp.transpose(attended, (1, 0, 2)).reshape(count, local_width)  10.8 us
  transfers between devices with their start and end apart: 2, of which 0 were waited for; matrix products, arithmetic and copies ran while one was open for 12% of the time, Pallas kernels for 0%

profile of v1, /device:TPU:0, one launch (start us, length us, event | category | flops | bytes accessed | tf_op | source)
XLA Modules:
  0.0 449.3 jit_solution(9760307638735278861)
XLA Ops:
  11.5 3.9 copy.79
  15.4 2.9 copy.82
  19.6 3.1 fusion.16
  24.8 69.2 %all-reduce = bf16[32]{0:T(256)(128)(2,1)S(1)} all-reduce(bf16[32]{0:T(256)(128)(2,1)S(1)} %dynamic-update-slice), channel_id=1, replica_groups=mesh['dp'=2,'seq'=32,'tensor'=2] {'seq'}, use_global_device_ids=true, to_apply=%add | all-reduce | flops 32 | bytes 128
  94.1 2.9 copy.78
  97.0 4.1 copy.87
  101.3 4.2 select_convert_fusion.1
  105.5 3.2 copy-done.1
  108.7 4.8 %fusion.40 = f32[16,512,128]{1,2,0:T(8,128)} fusion(bf16[16,512,512]{2,1,0:T(8,128)(2,1)S(1)} %select_convert_fusion.1, bf16[16,512,128]{1,2,0:T(8,128)(2,1)S(1)} %bitcast.108), kind=kOutput, calls=%fused_computation.72 | convolution fusion | flops 1073741824 | bytes 14680064 | tf_op jit(solution)/shard_map/hts,hsd->htd/dot_general | solution.py:100
  113.6 5.0 %fusion.7 = (f32[512]{0:T(512)S(1)}, f32[16,512,128]{1,2,0:T(8,128)}) fusion(f32[16,512,128]{1,2,0:T(8,128)} %fusion.40, f32[16,128,128]{2,1,0:T(8,128)S(1)} %get-tuple-element.133, pred[]{:T(512)S(6)} %not.3, bf16[16,512,128]{1,2,0:T(8,128)(2,1)S(1)} %bitcast.103, pred[512]{0:T(512)(128)(4,1)S(1)} %get-tuple-element.180), kind=kOutput, calls=%fused_computation.17 | convolution fusion | flops 272891392 | bytes 11536897 | tf_op jit(solution)/shard_map/htd,hde->hte/dot_general | solution.py:101
  118.6 5.0 %psum.28 = f32[512]{0:T(512)S(1)} all-reduce(f32[512]{0:T(512)S(1)} %get-tuple-element.183), channel_id=1, replica_groups=mesh['dp'=2,'seq'=32,'tensor'=2] {'tensor'}, use_global_device_ids=true, to_apply=%region_7.8 | all-reduce | flops 512 | bytes 4096 | tf_op jit(solution)/shard_map/psum | solution.py:105
  123.6 5.4 %copy.88 = f32[512,2048]{1,0:T(8,128)} copy(f32[512,2048]{0,1:T(8,128)} %bitcast.100) | data formatting | bytes 8388608 | tf_op jit(solution)/shard_map/reshape | solution.py:104
  129.0 4.0 fusion.2
  133.0 5.1 %psum.29 = f32[512]{0:T(512)S(1)} all-reduce(f32[512]{0:T(512)S(1)} %get-tuple-element.156), channel_id=1, replica_groups=mesh['dp'=2,'seq'=32,'tensor'=2] {'tensor'}, use_global_device_ids=true, to_apply=%region_9.10 | all-reduce | flops 512 | bytes 4096 | tf_op jit(solution)/shard_map/psum | solution.py:111
  138.2 4.3 fusion.8
  147.3 5.4 %copy.86 = f32[1,512,2048]{2,1,0:T(8,128)} copy(f32[1,512,2048]{1,2,0:T(8,128)} %bitcast.101) | data formatting | bytes 8388608 | tf_op jit(solution)/shard_map/reshape | solution.py:104
  152.7 4.8 %select_convert_fusion = bf16[16,512,512]{2,1,0:T(8,128)(2,1)S(1)} fusion(bf16[16,512,128]{1,2,0:T(8,128)(2,1)} %copy-done.7, bf16[16,512,128]{1,2,0:T(8,128)(2,1)} %bitcast.107, pred[512,512]{1,0:T(8,128)(4,1)S(1)} %fusion.24), kind=kOutput, calls=%fused_computation.4 | convolution fusion | flops 1082130432 | bytes 12845056 | tf_op jit(solution)/shard_map/hte,hse->hts/dot_general | solution.py:122
  157.6 4.8 %fusion.41 = f32[16,512,128]{1,2,0:T(8,128)} fusion(bf16[16,512,512]{2,1,0:T(8,128)(2,1)S(1)} %select_convert_fusion, bf16[16,512,128]{1,2,0:T(8,128)(2,1)S(1)} %bitcast.112), kind=kOutput, calls=%fused_computation.73 | convolution fusion | flops 1073741824 | bytes 14680064 | tf_op jit(solution)/shard_map/hts,hsd->htd/dot_general | solution.py:124
  162.4 4.3 add_convert_fusion.2
  166.7 3.9 copy.96
  170.6 7.0 %psum.30 = f32[2048]{0:T(1024)S(1)} all-reduce(f32[2048]{0:T(1024)S(1)} %get-tuple-element.155), channel_id=1, replica_groups=mesh['dp'=2,'seq'=32,'tensor'=2] {'dp'}, use_global_device_ids=true, to_apply=%region_14.15 | all-reduce | flops 2048 | bytes 16384 | tf_op jit(solution)/shard_map/psum | solution.py:13
  177.6 147.5 %psum.31 = f32[2048]{0:T(1024)} all-reduce(f32[2048]{0:T(1024)S(1)} %psum.30), channel_id=1, replica_groups=mesh['dp'=2,'seq'=32,'tensor'=2] {'seq'}, use_global_device_ids=true, to_apply=%region_15.16 | all-reduce | flops 2048 | bytes 16384 | tf_op jit(solution)/shard_map/psum | solution.py:14
  325.1 3.9 multiply_convert_fusion
  329.0 6.7 %fusion.42 = f32[16,512,128]{1,2,0:T(8,128)} fusion(bf16[16,512,128]{1,2,0:T(8,128)(2,1)S(1)} %bitcast.105, bf16[16,512,512]{2,1,0:T(8,128)(2,1)} %copy-done), kind=kOutput, calls=%fused_computation.74 | convolution fusion | flops 1073741824 | bytes 14680064 | tf_op jit(solution)/shard_map/hts,htd->hsd/dot_general | solution.py:128
  335.8 86.6 %while.27 = (s32[]{:T(128)}, f32[16,128,128]{2,1,0:T(8,128)S(1)}, s32[]{:T(128)}, bf16[32,16,128,128]{3,2,1,0:T(8,128)(2,1)}, bf16[32,1]{0,1:T(2,128)(2,1)S(1)},...) while((s32[]{:T(128)}, f32[16,128,128]{2,1,0:T(8,128)S(1)}, s32[]{:T(128)}, ...), condition=%wide.region_12.13_spmd, body=%wide.region_11.12_spmd.sunk | while | flops 786439 | bytes 2621605 | solution.py:40
  336.5 2.1 convert_add_fusion.5
  339.3 2.1 convert_add_fusion.5
  342.1 2.1 convert_add_fusion.5
  344.8 2.1 convert_add_fusion.5
  347.6 2.1 convert_add_fusion.5
  350.4 2.1 convert_add_fusion.5
  353.2 2.1 convert_add_fusion.5
  356.0 2.1 convert_add_fusion.5
  358.8 2.1 convert_add_fusion.5
  361.6 2.1 convert_add_fusion.5
  364.4 2.1 convert_add_fusion.5
  367.1 2.1 convert_add_fusion.5
  369.9 2.1 convert_add_fusion.5
  372.7 2.1 convert_add_fusion.5
  375.5 2.1 convert_add_fusion.5
  378.3 2.1 convert_add_fusion.5
  381.1 2.1 convert_add_fusion.5
  383.9 2.1 convert_add_fusion.5
  386.7 2.1 convert_add_fusion.5
  424.0 6.2 %add_convert_fusion = bf16[16,512,128]{1,2,0:T(8,128)(2,1)} fusion(f32[16,512,128]{1,2,0:T(8,128)S(1)} %fusion.14, bf16[16,512,128]{1,2,0:T(8,128)(2,1)S(1)} %copy-done.9, bf16[16,512,512]{2,1,0:T(8,128)(2,1)} %copy-done.1), kind=kOutput, calls=%fused_computation.18 | convolution fusion | flops 1075838976 | bytes 16777216 | tf_op jit(solution)/shard_map/hts,hte->hse/dot_general | solution.py:132
  430.3 4.1 copy.98
  434.3 4.2 add_convert_fusion.1
  438.6 3.9 copy.97
  (94 shorter events, 58.3 us)
Async XLA Ops:
  7.2 106.3 %all-gather.5.cloned.1.call-start = ((), (), s32[]{:S(2)}) async-start(), calls=%async_computation | async-start | bytes 17301504 | tf_op jit(solution)/shard_map/all_gather | solution.py:25
  18.3 4.5 copy-start.2
  19.6 3.9 copy-start.11
  22.8 312.9 %all-gather.7.cloned.1.call-start = ((), (), s32[]{:S(2)}) async-start(), calls=%async_computation.1 | async-start | bytes 17301504 | tf_op jit(solution)/shard_map/all_gather | solution.py:25
  101.3 7.4 %copy-start.3 = (bf16[1,512,2048]{1,2,0:T(8,128)(2,1)S(1)}, bf16[1,512,2048]{1,2,0:T(8,128)(2,1)}, u32[]{:S(2)}) copy-start(bf16[1,512,2048]{1,2,0:T(8,128)(2,1)} %copy-done.2) | copy-start | bytes 6291460
  105.5 3.2 copy-start.1
  123.6 5.4 %copy-start.10 = (f32[2048]{0:T(1024)S(1)}, f32[2048]{0:T(1024)}, u32[]{:S(2)}) copy-start(f32[2048]{0:T(1024)} %param.15) | copy-start | bytes 24580
  142.4 1.4 copy-start.7
  152.7 4.8 %copy-start.5 = (bf16[1,512,2048]{1,2,0:T(8,128)(2,1)S(1)}, bf16[1,512,2048]{1,2,0:T(8,128)(2,1)}, u32[]{:S(2)}) copy-start(bf16[1,512,2048]{1,2,0:T(8,128)(2,1)} %copy.79) | copy-start | bytes 6291460
  157.6 4.8 %copy-start = (bf16[16,512,512]{2,1,0:T(8,128)(2,1)}, bf16[16,512,512]{2,1,0:T(8,128)(2,1)S(1)}, u32[]{:S(2)}) copy-start(bf16[16,512,512]{2,1,0:T(8,128)(2,1)S(1)} %select_convert_fusion) | copy-start | bytes 25165828
  157.6 4.8 %copy-start.8 = (bf16[16,512,128]{1,2,0:T(8,128)(2,1)S(1)}, bf16[16,512,128]{1,2,0:T(8,128)(2,1)}, u32[]{:S(2)}) copy-start(bf16[16,512,128]{1,2,0:T(8,128)(2,1)} %copy-done.7) | copy-start | bytes 6291460
  335.8 86.7 %copy-start.6 = (bf16[1,512,2048]{1,2,0:T(8,128)(2,1)S(1)}, bf16[1,512,2048]{1,2,0:T(8,128)(2,1)}, u32[]{:S(2)}) copy-start(bf16[1,512,2048]{1,2,0:T(8,128)(2,1)} %copy.79) | copy-start | bytes 6291460
  422.5 1.6 copy-start.9
  430.3 4.1 copy-start.4
Sparse Core Ops, SparseCore 0:
  22.9 75.2 all-gather.4
  145.5 151.5 all-gather.6
